TPU v7x, 32 devices: a whole 2x2x4 slice. The times are simulated.
32 devices in a mesh: row: 2 (over core), col: 4 (over z), kk: 4 (over y, x).
Axes of the slice: x: 2, y: 2, z: 4, core: 2. Of those that a mesh axis runs over, the one named last changes fastest.
Arguments:
- contribution: float32 [32, 256, 16, 512], P('kk', 'row', None, 'col'), may hold values from -6 to 6
- left_panel: float32 [32, 256, 4, 768], P(None, 'row', 'kk', 'col'), may hold values from -6 to 6
- right_panel: float32 [4, 768, 16, 512], P('kk', 'row', None, 'col'), may hold values from -0.109375 to 0.109375
Outputs:
- updated: float32 [32, 256, 16, 512], P('kk', 'row', None, 'col')
All inputs are finite; a program needn't handle non-finite values.
Results may differ from a plain program's by a relative error of at most 0.00005.
Values sent between devices are 32-bit elements; how exact they have to be, the bound alone decides.
No kernel may reach another device: no remote copies, remote signals or barrier semaphores. Data moves between devices by JAX's collectives and lax.ppermute only.
A program may use at most 128 MiB of HBM per device.

v0:
```python
import jax
import jax.numpy as jnp
from jax import lax
from jax.sharding import PartitionSpec as P


def local(contribution, left_panel, right_panel):
    right_rows = lax.all_gather(right_panel, "row", axis=1, tiled=True)
    col_width = contribution.shape[2] * contribution.shape[3]
    exchanged = lax.all_to_all(left_panel, "kk", split_axis=0, concat_axis=2, tiled=True)
    left_full = lax.all_gather(exchanged, "col", axis=3, tiled=True)
    right_full = lax.all_gather(right_rows, "kk", axis=0, tiled=True)
    row_total = left_full.shape[0] * left_full.shape[1]
    left_flat = left_full.reshape(row_total, -1)
    right_flat = right_full.reshape(-1, col_width)
    product = jnp.dot(
        left_flat, right_flat, precision=lax.Precision.HIGHEST, preferred_element_type=jnp.float32
    )
    product = product.reshape(contribution.shape)
    return contribution - product


def solution(mesh):
    placed = (P("kk", "row", None, "col"), P(None, "row", "kk", "col"), P("kk", "row", None, "col"))
    return jax.shard_map(
        local, mesh=mesh, in_specs=placed, out_specs=P("kk", "row", None, "col"), check_vma=False
    )
```

profile of v0, /device:TPU:0, one launch (start us, length us, event | category | flops | bytes accessed | tf_op | source)
XLA Modules:
  0.0 655.1 jit_solution(10757515280889346965)
XLA Ops:
  6.5 0.0 all-gather.5.cloned.1.call-start
  6.5 0.7 all-gather.5.cloned.1.call-update
  7.3 0.0 all-gather.9.cloned.1.call-start
  7.3 41.9 %all_to_all.18 = f32[32,128,1,192]{1,3,2,0:T(8,128)S(1)} all-to-all(f32[32,128,1,192]{1,3,2,0:T(8,128)} %param.4), channel_id=1, replica_groups=mesh['row'=2,'col'=4,'kk'=4] {'kk'}, dimensions={0} | all-to-all | bytes 6291456 | tf_op jit(solution)/shard_map/all_to_all | solution.py:10
  49.2 3.5 copy.21
  52.6 0.0 all-gather.9.cloned.1.call-update
  52.7 0.0 all-gather.7.cloned.1.call-start
  52.7 0.0 all-gather.5.cloned.1.call-done
  52.7 0.7 all-gather.7.cloned.1.call-update
  53.4 217.5 %all-gather.9.cloned.1.call-done = f32[8,128,4,1,768]{1,0,3,2,4:T(8,128)} async-done(((f32[8,128,4,1,192]{1,0,3,2,4:T(8,128)}), f32[8,128,4,1,768]{1,0,3,2,4:T(8,128)}) %all-gather.9.cloned.1.call-update) | async-done | bytes 12582928 | tf_op jit(solution)/shard_map/all_gather | solution.py:11
  270.9 14.2 %copy.9 = f32[8,128,4,1,768]{4,2,1,0,3:T(4,128)} copy(f32[8,128,4,1,768]{1,0,3,2,4:T(8,128)} %all-gather.9.cloned.1.call-done) | data formatting | bytes 25165824 | tf_op jit(solution)/shard_map/all_gather | solution.py:11
  285.1 16.0 %reshape.11 = f32[8,128,3072,1]{2,1,0,3:T(8,128)} reshape(f32[8,128,4,1,768]{4,2,1,0,3:T(4,128)} %copy.9) | data formatting | bytes 25165824 | tf_op jit(solution)/shard_map/dot_general | solution.py:16
  301.1 197.5 %all-gather.7.cloned.1.call-done = f32[4,768,16,128]{3,2,1,0:T(8,128)} async-done(((f32[1,768,16,128]{3,2,1,0:T(8,128)}), f32[4,768,16,128]{3,2,1,0:T(8,128)}) %all-gather.7.cloned.1.call-update) | async-done | bytes 25165840 | tf_op jit(solution)/shard_map/all_gather | solution.py:12
  498.6 22.8 %copy.20 = f32[384,8,16,128]{3,1,2,0:T(8,128)} copy(f32[384,8,16,128]{3,2,1,0:T(8,128)} %bitcast.26) | data formatting | bytes 50331648
  521.4 24.8 %copy.12 = f32[3072,2048]{0,1:T(8,128)} copy(f32[3072,2048]{1,0:T(8,128)} %bitcast.25) | data formatting | bytes 50331648 | tf_op jit(solution)/shard_map/reshape | solution.py:15
  546.2 90.9 %copy_subtract_fusion = f32[8,128,16,128]{3,1,2,0:T(8,128)} fusion(f32[8,128,16,128]{3,2,1,0:T(8,128)} %param.3, f32[16,128,3072,1]{2,1,0,3:T(8,128)} %bitcast.27, f32[8,128,3072,1]{2,1,0,3:T(8,128)} %reshape.11), kind=kOutput, calls=%fused_computation.3 | convolution fusion | flops 77311508480 | bytes 54525952 | tf_op jit(solution)/shard_map/dot_general | solution.py:16
  637.0 11.5 %copy.14 = f32[8,128,16,128]{3,2,1,0:T(8,128)} copy(f32[8,128,16,128]{3,1,2,0:T(8,128)} %copy_subtract_fusion) | data formatting | bytes 16777216 | tf_op jit(solution)/shard_map/sub | solution.py:20
Async XLA Ops:
  6.5 46.2 %all-gather.5.cloned.1.call-start = ((), (), s32[]{:S(2)}) async-start(), calls=%async_computation.1 | async-start | bytes 9437184 | tf_op jit(solution)/shard_map/all_gather | solution.py:8
  7.3 263.7 %all-gather.9.cloned.1.call-start = ((), (), s32[]{:S(2)}) async-start(), calls=%async_computation.3 | async-start | bytes 15728640 | tf_op jit(solution)/shard_map/all_gather | solution.py:11
  52.7 445.9 %all-gather.7.cloned.1.call-start = ((), (), s32[]{:S(2)}) async-start(), calls=%async_computation.2 | async-start | bytes 31457280 | tf_op jit(solution)/shard_map/all_gather | solution.py:12
Sparse Core Ops, SparseCore 0:
  8.9 19.4 all-gather.4
  52.8 218.0 all-gather.8
  272.8 225.7 all-gather.6
where the time goes:
time: 656 us; the launch traced here: 655 us
  waiting for transfers between devices  416 us (63%)
  local copies, waits for them, and re-layouts  92.8 us (14%)
  matrix products  90.9 us (14%)
  blocking collectives  41.9 us (6%)
  between operations  13.1 us (2%)
    all_gather x1, waiting for transfers between devices, local(): left_full = lax.all_gather(exchanged, 'col', axis=3, tiled=True)  218 us
    all_gather x1, waiting for transfers between devices, local(): right_full = lax.all_gather(right_rows, 'kk', axis=0, tiled=True)  197 us
    dot_general x1, matrix products, local(): jnp.dot(left_flat, right_flat, precision=lax.Precision.HIGHEST, preferred...  90.9 us
    all_to_all x1, blocking collectives, local(): lax.all_to_all(left_panel, 'kk', split_axis=0, concat_axis=2, tiled=True)  41.9 us
    reshape x1, local copies, waits for them, and re-layouts, local(): right_flat = right_full.reshape(-1, col_width)  24.8 us
    unnamed x1, local copies, waits for them, and re-layouts  22.8 us
    dot_general x1, local copies, waits for them, and re-layouts, local(): jnp.dot(left_flat, right_flat, precision=lax.Precision.HIGHEST, preferred...  16 us
    all_gather x1, local copies, waits for them, and re-layouts, local(): left_full = lax.all_gather(exchanged, 'col', axis=3, tiled=True)  14.2 us
  transfers between devices with their start and end apart: 3, of which 2 were waited for; matrix products, arithmetic and copies ran while one was open for 5% of the time, Pallas kernels for 0%

commit v1 on v0

--- a/solution.py
+++ b/solution.py
@@ -1,14 +1,27 @@
+import functools
 import jax
 import jax.numpy as jnp
 from jax import lax
 from jax.sharding import PartitionSpec as P
 
 
+def extend_units_on_mesh(block_here, net_axis):
+    return jnp.concatenate(
+        lax.all_to_all(
+            jnp.stack([block_here for _ in range(lax.axis_size(net_axis))]), net_axis, 0, 0
+        ),
+        axis=3,
+    )
+
+
+write_node = functools.partial(extend_units_on_mesh, net_axis="col")
+
+
 def local(contribution, left_panel, right_panel):
     right_rows = lax.all_gather(right_panel, "row", axis=1, tiled=True)
     col_width = contribution.shape[2] * contribution.shape[3]
     exchanged = lax.all_to_all(left_panel, "kk", split_axis=0, concat_axis=2, tiled=True)
-    left_full = lax.all_gather(exchanged, "col", axis=3, tiled=True)
+    left_full = write_node(exchanged)
     right_full = lax.all_gather(right_rows, "kk", axis=0, tiled=True)
     row_total = left_full.shape[0] * left_full.shape[1]
     left_flat = left_full.reshape(row_total, -1)

time: 656 us -> 613 us (0.934)
  waiting for transfers between devices: 416 us -> 21.8 us
  blocking collectives: 41.9 us -> 338 us
  matrix products: 90.9 us -> 167 us
  local copies, waits for them, and re-layouts: 92.8 us -> 71.6 us
    all_to_all x0 -> x1, blocking collectives: none -> 276 us  [extend_units_on_mesh(): lax.all_to_all(jnp.stack([block_here for _ in range(lax.axis_size(net_axi...]
    all_gather x1 -> x0, waiting for transfers between devices: 218 us -> none  [local(): left_full = lax.all_gather(exchanged, 'col', axis=3, tiled=True)]
    all_gather x1, waiting for transfers between devices: 197 us -> 0.01 us  [local(): right_full = lax.all_gather(right_rows, 'kk', axis=0, tiled=True)]
    dot_general x1, matrix products: 90.9 us -> 167 us  [local(): jnp.dot(left_flat, right_flat, precision=lax.Precision.HIGHEST, preferred...]
    all_gather x1, waiting for transfers between devices: 0.02 us -> 21.1 us  [local(): right_rows = lax.all_gather(right_panel, 'row', axis=1, tiled=True)]
    all_to_all x1, blocking collectives: 41.9 us -> 62.1 us  [local(): lax.all_to_all(left_panel, 'kk', split_axis=0, concat_axis=2, tiled=True)]
    dot_general x1 -> x0, local copies, waits for them, and re-layouts: 16 us -> none  [local(): jnp.dot(left_flat, right_flat, precision=lax.Precision.HIGHEST, preferred...]
    all_gather x1 -> x0, local copies, waits for them, and re-layouts: 14.2 us -> none  [local(): left_full = lax.all_gather(exchanged, 'col', axis=3, tiled=True)]
  transfers between devices with their start and end apart: 3 -> 2, of which waited for: 2 -> 1; matrix products, arithmetic and copies ran while one was open for 5% -> 2% of each run, Pallas kernels for 0% -> 0%
where the time goes in v1:
time: 613 us; the launch traced here: 612 us
  blocking collectives  338 us (55%)
  matrix products  167 us (27%)
  local copies, waits for them, and re-layouts  71.6 us (12%)
  waiting for transfers between devices  21.8 us (4%)
  between operations  13.4 us (2%)
    all_to_all x1, blocking collectives, extend_units_on_mesh(): lax.all_to_all(jnp.stack([block_here for _ in range(lax.axis_size(net_axi...  276 us
    dot_general x1, matrix products, local(): jnp.dot(left_flat, right_flat, precision=lax.Precision.HIGHEST, preferred...  167 us
    all_to_all x1, blocking collectives, local(): lax.all_to_all(left_panel, 'kk', split_axis=0, concat_axis=2, tiled=True)  62.1 us
    reshape x1, local copies, waits for them, and re-layouts, local(): right_flat = right_full.reshape(-1, col_width)  24.7 us
    unnamed x1, local copies, waits for them, and re-layouts  22.8 us
    all_gather x1, waiting for transfers between devices, local(): right_rows = lax.all_gather(right_panel, 'row', axis=1, tiled=True)  21.1 us
  transfers between devices with their start and end apart: 2, of which 1 were waited for; matrix products, arithmetic and copies ran while one was open for 2% of the time, Pallas kernels for 0%

profile of v1, /device:TPU:0, one launch (start us, length us, event | category | flops | bytes accessed | tf_op | source)
XLA Modules:
  0.0 611.8 jit_solution(6363126512765457398)
XLA Ops:
  6.5 0.0 all-gather.3.cloned.1.call-start
  6.5 0.7 all-gather.3.cloned.1.call-update
  7.3 0.0 all-gather.5.cloned.1.call-start
  7.3 21.1 %all-gather.3.cloned.1.call-done = f32[1,768,16,128]{3,2,0,1:T(8,128)} async-done(((f32[1,384,16,128]{3,2,0,1:T(8,128)}), f32[1,768,16,128]{3,2,0,1:T(8,128)}) %all-gather.3.cloned.1.call-update) | async-done | bytes 6291472 | tf_op jit(solution)/shard_map/all_gather | solution.py:21
  28.4 0.0 all-gather.5.cloned.1.call-update
  28.4 62.1 %all_to_all.20 = f32[32,128,1,192]{1,3,2,0:T(8,128)S(1)} all-to-all(f32[32,128,1,192]{1,3,2,0:T(8,128)} %param.4), channel_id=1, replica_groups=mesh['row'=2,'col'=4,'kk'=4] {'kk'}, dimensions={0} | all-to-all | bytes 6291456 | tf_op jit(solution)/shard_map/all_to_all | solution.py:23
  90.5 0.3 copy.29
  90.9 1.6 stack.10
  92.4 276.0 %all_to_all.21 = f32[4,8,128,4,192]{2,4,3,1,0:T(8,128)} all-to-all(f32[4,8,128,4,192]{2,4,3,1,0:T(8,128)S(1)} %stack.10), channel_id=1, replica_groups=mesh['row'=2,'col'=4,'kk'=4] {'col'}, dimensions={0} | all-to-all | bytes 25165824 | tf_op jit(solution)/shard_map/all_to_all | solution.py:10
  368.5 10.7 %copy.14 = f32[4,8,128,4,192]{2,4,0,3,1:T(8,128)} copy(f32[4,8,128,4,192]{2,4,3,1,0:T(8,128)} %all_to_all.21) | data formatting | bytes 25165824 | tf_op jit(solution)/shard_map/all_to_all | solution.py:10
  379.2 0.0 all-gather.5.cloned.1.call-done
  379.2 22.8 %copy.28 = f32[384,8,16,128]{3,1,2,0:T(8,128)} copy(f32[384,8,16,128]{3,2,1,0:T(8,128)} %bitcast.28) | data formatting | bytes 50331648
  402.0 24.7 %copy.17 = f32[3072,2048]{0,1:T(8,128)} copy(f32[3072,2048]{1,0:T(8,128)} %bitcast.27) | data formatting | bytes 50331648 | tf_op jit(solution)/shard_map/reshape | solution.py:28
  426.7 166.8 %copy_subtract_fusion = f32[8,128,16,128]{3,1,2,0:T(8,128)} fusion(f32[8,128,16,128]{3,2,1,0:T(8,128)} %param.3, f32[8,128,3072,1]{1,2,3,0:T(8,128)} %bitcast.30, f32[16,128,3072,1]{2,1,0,3:T(8,128)} %bitcast.29), kind=kOutput, calls=%fused_computation.1 | convolution fusion | flops 77311508480 | bytes 54525952 | tf_op jit(solution)/shard_map/dot_general | solution.py:29
  593.5 11.5 %copy.20 = f32[8,128,16,128]{3,2,1,0:T(8,128)} copy(f32[8,128,16,128]{3,1,2,0:T(8,128)} %copy_subtract_fusion) | data formatting | bytes 16777216 | tf_op jit(solution)/shard_map/sub | solution.py:33
Async XLA Ops:
  6.5 21.8 %all-gather.3.cloned.1.call-start = ((), (), s32[]{:S(2)}) async-start(), calls=%async_computation.2 | async-start | bytes 9437184 | tf_op jit(solution)/shard_map/all_gather | solution.py:21
  7.3 371.9 %all-gather.5.cloned.1.call-start = ((), (), s32[]{:S(2)}) async-start(), calls=%async_computation.3 | async-start | bytes 31457280 | tf_op jit(solution)/shard_map/all_gather | solution.py:25
Sparse Core Ops, SparseCore 0:
  8.9 19.4 all-gather.2
  30.2 248.9 all-gather.4
